TPU v7x, 32 devices: a whole 2x2x4 slice. The times are simulated.
32 devices in a mesh: grp: 4 (over x, core), rep: 8 (over z, y).
Axes of the slice: x: 2, y: 2, z: 4, core: 2. Of those that a mesh axis runs over, the one named last changes fastest.
Arguments:
- particles: bfloat16 [8192, 64, 256], P(('grp', 'rep')), may hold values from -6 to 6
- noise_var: float32 [8192], P(('grp', 'rep')), may hold values from 32 to 800
- references: bfloat16 [200, 64, 256], P('grp', 'rep'), may hold values from -6 to 6
- class_order: int32 [200], replicated, may hold values from 0 to 199, as said below
- candidates: int32 [32, 8], P(('grp', 'rep')), may hold values from 0 to 199, as said below
Outputs:
- class_sums: float32 [200, 64, 256], P('grp', 'rep')
- class_weights: float32 [200], P('grp')
Inputs may be any that keep to these rules, and one draw needn't show every extreme that they name: `class_order`: a permutation; the slots of index g of grp are g * 50 to g * 50 + 49. `candidates`: each row names 8 different classes, whose slots lie with 4 indices of grp, exactly 2 with each.
All inputs are finite; a program needn't handle non-finite values.
Results may differ from a plain program's by a relative error of at most 0.0024.
Values may be sent and summed in bfloat16 or wider, within the bound.
A program may use at most 128 MiB of HBM per device.

v0:
```python
import functools
import math

import jax
import jax.numpy as jnp
import numpy as np
from jax import lax
from jax.experimental import pallas as pl
from jax.experimental.pallas import tpu as pltpu
from jax.sharding import PartitionSpec as P

precise = lax.Precision.HIGHEST
GROUP = 16
OWN = 2


def angle_tables(freq_count, angle_count):
    product = np.arange(freq_count)[:, None] * np.arange(angle_count)[None, :] % angle_count
    phase_angle = product * (2.0 * math.pi / angle_count)
    return np.cos(phase_angle).astype(np.float32), np.sin(phase_angle).astype(np.float32)


def peer_of(step, n_rep, total):
    me = lax.axis_index("grp") * n_rep + lax.axis_index("rep")
    peer = lax.rem(me + step, total)
    return peer, {"grp": peer // n_rep, "rep": lax.rem(peer, n_rep)}


def greet_all(n_rep, total):
    barrier = pltpu.get_barrier_semaphore()

    @pl.loop(1, total)
    def _(step):
        _, where = peer_of(step, n_rep, total)
        pl.semaphore_signal(
            barrier, inc=1, device_id=where, device_id_type=pl.DeviceIdType.MESH
        )


def await_all(total):
    pl.semaphore_wait(pltpu.get_barrier_semaphore(), total - 1)


def remote(src, dst, send_sem, recv_sem, where):
    return pltpu.make_async_remote_copy(
        src_ref=src,
        dst_ref=dst,
        send_sem=send_sem,
        recv_sem=recv_sem,
        device_id=where,
        device_id_type=pl.DeviceIdType.MESH,
    )


def relayout_blocks(
    rows_ref, major_ref, in_buf, mid_buf, out_buf, in_sem, out_sem, start, stop
):
    half = rows_ref.shape[2] // 2

    def load(block):
        slot = lax.rem(block, 2)
        return pltpu.make_async_copy(
            rows_ref.at[pl.ds(block * GROUP, GROUP)], in_buf.at[slot], in_sem.at[slot]
        )

    def store(block):
        slot = lax.rem(block, 2)
        return pltpu.make_async_copy(
            out_buf.at[slot],
            major_ref.at[:, pl.ds(pl.multiple_of(block * GROUP, GROUP), GROUP), :],
            out_sem.at[slot],
        )

    load(start).start()

    @pl.loop(start, stop)
    def _(block):
        slot = lax.rem(block, 2)

        @pl.when(block + 1 < stop)
        def _():
            load(block + 1).start()

        load(block).wait()

        @pl.when(block >= start + 2)
        def _():
            store(block - 2).wait()

        for p in range(GROUP):
            both = jnp.concatenate(
                [in_buf[slot, p, :, :half], in_buf[slot, p, :, half:]], axis=0
            )
            mid_buf[pl.ds(p, half, stride=GROUP), :] = both.T.astype(jnp.float32)
        out_buf[slot] = mid_buf[...].reshape(out_buf.shape[1:]).astype(out_buf.dtype)
        store(block).start()

    store(stop - 2).wait()
    store(stop - 1).wait()


def fetch_kernel(
    n_rep,
    total,
    cand_ref,
    order_ref,
    refs_ref,
    rows_ref,
    got_ref,
    slots_ref,
    major_ref,
    cand_pad,
    cand_all,
    slot_vec,
    slot_smem,
    send_buf,
    c_send,
    c_recv,
    d_send,
    d_recv,
    l_sem,
    in_buf,
    mid_buf,
    out_buf,
    in_sem,
    out_sem,
):
    grp = lax.axis_index("grp")
    me = grp * n_rep + lax.axis_index("rep")
    owned = refs_ref.shape[0]
    cand_pad[...] = jnp.full(cand_pad.shape, -1, jnp.int32)
    cand_pad[:, : cand_ref.shape[1]] = cand_ref[...]
    greet_all(n_rep, total)
    relayout = functools.partial(
        relayout_blocks, rows_ref, major_ref, in_buf, mid_buf, out_buf, in_sem, out_sem
    )
    blocks = rows_ref.shape[0] // GROUP
    cut_one, cut_two = blocks // 4, blocks // 2
    relayout(0, cut_one)
    await_all(total)

    def cand_copy(step, slot):
        _, where = peer_of(step, n_rep, total)
        return remote(cand_pad, cand_all.at[slot], c_send.at[step], c_recv.at[slot], where)

    @pl.loop(1, total)
    def _(step):
        cand_copy(step, me).start()

    cand_all[me] = cand_pad[...]
    relayout(cut_one, cut_two)

    @pl.loop(1, total)
    def _(step):
        cand_copy(step, peer_of(step, n_rep, total)[0]).wait_recv()

    order = order_ref[...]
    slot_no = lax.broadcasted_iota(jnp.int32, (1, order.shape[1]), 1) - grp * owned
    mine = jnp.where((slot_no >= 0) & (slot_no < owned), order, -2)
    cands = cand_all[...].reshape(total, cand_all.shape[2])
    hit = cands[:, 0:1] == mine
    for j in range(1, cand_ref.shape[1]):
        hit = jnp.logical_or(hit, cands[:, j : j + 1] == mine)
    first = jnp.min(jnp.where(hit, slot_no, 2 * owned), axis=1, keepdims=True)
    last = jnp.max(jnp.where(hit, slot_no, -1), axis=1, keepdims=True)
    lane = lax.broadcasted_iota(jnp.int32, slots_ref.shape, 1)
    slots_ref[...] = jnp.where(lane == 0, first, last)
    slot_vec[...] = jnp.where(
        lane == 0, jnp.minimum(first, owned - 1), jnp.maximum(last, 0)
    )
    to_scalar = pltpu.make_async_copy(slot_vec, slot_smem, l_sem.at[0])
    to_scalar.start()
    to_scalar.wait()

    def data_copy(step, block, slot):
        _, where = peer_of(step, n_rep, total)
        return remote(
            send_buf.at[block], got_ref.at[slot], d_send.at[step], d_recv.at[slot], where
        )

    @pl.loop(1, total)
    def _(step):
        peer, _ = peer_of(step, n_rep, total)
        for i in range(OWN):
            send_buf[peer, i] = refs_ref[slot_smem[peer, i]]
        data_copy(step, peer, me).start()

    for i in range(OWN):
        got_ref[me, i] = refs_ref[slot_smem[me, i]]

    relayout(cut_two, blocks)

    @pl.loop(1, total)
    def _(step):
        peer, _ = peer_of(step, n_rep, total)
        cand_copy(step, me).wait_send()
        data_copy(step, peer, peer).wait()


def fetch(cand, order, refs, rows, n_rep, total):
    count, depth, full = rows.shape
    half = full // 2
    owned, cycles, width = refs.shape
    vmem = pl.BlockSpec(memory_space=pltpu.VMEM)
    return pl.pallas_call(
        functools.partial(fetch_kernel, n_rep, total),
        out_shape=(
            jax.ShapeDtypeStruct((total, OWN, cycles, width), refs.dtype),
            jax.ShapeDtypeStruct((total, 128), jnp.int32),
            jax.ShapeDtypeStruct((half, count, 2 * depth), rows.dtype),
        ),
        in_specs=[vmem] * 3 + [pl.BlockSpec(memory_space=pl.ANY)],
        out_specs=(vmem, vmem, pl.BlockSpec(memory_space=pl.ANY)),
        scratch_shapes=[
            pltpu.VMEM((1, 128), jnp.int32),
            pltpu.VMEM((total, 1, 128), jnp.int32),
            pltpu.VMEM((total, 128), jnp.int32),
            pltpu.SMEM((total, 128), jnp.int32),
            pltpu.VMEM((total, OWN, cycles, width), refs.dtype),
            pltpu.SemaphoreType.DMA((total,)),
            pltpu.SemaphoreType.DMA((total,)),
            pltpu.SemaphoreType.DMA((total,)),
            pltpu.SemaphoreType.DMA((total,)),
            pltpu.SemaphoreType.DMA((1,)),
            pltpu.VMEM((2, GROUP, depth, full), rows.dtype),
            pltpu.VMEM((half * GROUP, 2 * depth), jnp.float32),
            pltpu.VMEM((2, half, GROUP, 2 * depth), rows.dtype),
            pltpu.SemaphoreType.DMA((2,)),
            pltpu.SemaphoreType.DMA((2,)),
        ],
        compiler_params=pltpu.CompilerParams(collective_id=0, has_side_effects=True),
        name="fetch",
    )(cand, order, refs, rows)


def return_kernel(
    n_rep, total, sums_ref, weight_ref, got_ref, got_w_ref, s_send, s_recv, w_send, w_recv, l_sem
):
    grp = lax.axis_index("grp")
    rep = lax.axis_index("rep")
    me = grp * n_rep + rep
    greet_all(n_rep, total)
    await_all(total)

    def copies(step, slot):
        _, where = peer_of(step, n_rep, total)
        return (
            remote(
                sums_ref.at[where["grp"], where["rep"]],
                got_ref.at[slot],
                s_send.at[step],
                s_recv.at[slot],
                where,
            ),
            remote(
                weight_ref.at[where["grp"]],
                got_w_ref.at[slot],
                w_send.at[step],
                w_recv.at[slot],
                where,
            ),
        )

    @pl.loop(1, total)
    def _(step):
        for copy in copies(step, me):
            copy.start()

    got_ref[me] = sums_ref[grp, rep]
    got_w_ref[me] = weight_ref[grp]

    @pl.loop(1, total)
    def _(step):
        for copy in copies(step, peer_of(step, n_rep, total)[0]):
            copy.wait()


def give_back(sums, weight, n_rep, total):
    vmem = pl.BlockSpec(memory_space=pltpu.VMEM)
    return pl.pallas_call(
        functools.partial(return_kernel, n_rep, total),
        out_shape=(
            jax.ShapeDtypeStruct((total,) + sums.shape[2:], sums.dtype),
            jax.ShapeDtypeStruct((total,) + weight.shape[1:], weight.dtype),
        ),
        in_specs=[vmem] * 2,
        out_specs=(vmem, vmem),
        scratch_shapes=[
            pltpu.SemaphoreType.DMA((total,)),
            pltpu.SemaphoreType.DMA((total,)),
            pltpu.SemaphoreType.DMA((total,)),
            pltpu.SemaphoreType.DMA((total,)),
            pltpu.SemaphoreType.DMA((1,)),
        ],
        compiler_params=pltpu.CompilerParams(collective_id=1, has_side_effects=True),
        name="give_back",
    )(sums, weight)


def split_wide(value):
    high = value.astype(jnp.bfloat16)
    return high, (value - high.astype(jnp.float32)).astype(jnp.bfloat16)


def dot_wide(left, right, precision=None):
    return jnp.dot(left, right, precision=precision, preferred_element_type=jnp.float32)


def terms_kernel(
    major_ref,
    q_ref,
    angles_ref,
    freqs_ref,
    noise_ref,
    norm_ref,
    numer_ref,
    weight_ref,
    x_buf,
    f_buf,
    t_buf,
    x_sem,
):
    half, rows, depth = major_ref.shape
    both = q_ref.shape[1]
    cands = both // 2
    width = 2 * half
    cycles = depth // 2
    chunks = x_sem.shape[0]
    span = half // chunks

    lanes = f_buf.shape[2]
    tiles = range(f_buf.shape[0])

    def take(part):
        return jnp.concatenate([f_buf[t, part, :] for t in tiles], axis=1)

    def put(part, value):
        for t in tiles:
            f_buf[t, part, :] = value[:, t * lanes : (t + 1) * lanes]

    def chunk_copy(chunk):
        part = pl.ds(chunk * span, span)
        return pltpu.make_async_copy(major_ref.at[part], x_buf.at[part], x_sem.at[chunk])

    for chunk in range(chunks):
        chunk_copy(chunk).start()

    for chunk in range(chunks):
        chunk_copy(chunk).wait()

        @pl.loop(chunk * span, (chunk + 1) * span, unroll=8)
        def _(k):
            found = lax.dot_general(
                q_ref[k],
                x_buf[k],
                (((1,), (1,)), ((), ())),
                preferred_element_type=jnp.float32,
            )
            put(pl.ds(k, both, stride=half), found)

    inv_noise = 1.0 / noise_ref[...]
    top = jnp.full((1, rows), -jnp.inf, jnp.float32)
    for j in range(cands):
        part = pl.ds(j * width, width)
        correlation = dot_wide(angles_ref[...], take(part), precise)
        logits = (correlation - norm_ref[j : j + 1, :]) * inv_noise
        put(part, logits)
        top = jnp.maximum(top, jnp.max(logits, axis=0, keepdims=True))

    sums = []
    for j in range(cands):
        part = pl.ds(j * width, width)
        exponent = jnp.exp(take(part) - top)
        put(part, exponent)
        sums.append(jnp.sum(exponent, axis=0, keepdims=True))
    inv_sum = 1.0 / sum(sums)
    freqs_high, freqs_low = split_wide(freqs_ref[...])
    for j in range(cands):
        part = pl.ds(j * width, width)
        weight = jnp.sum(sums[j] * inv_sum, axis=1, keepdims=True)
        weight_ref[j : j + 1, :] = jnp.broadcast_to(weight, (1, weight_ref.shape[1]))
        high, low = split_wide(take(part) * inv_sum)
        put(
            part,
            dot_wide(freqs_high, high) + dot_wide(freqs_low, high) + dot_wide(freqs_high, low),
        )

    @pl.loop(0, half, unroll=8)
    def _(k):
        spectra = take(pl.ds(k, both, stride=half)).astype(jnp.bfloat16)
        t_buf[pl.ds(k, both, stride=half), :] = dot_wide(spectra, x_buf[k])

    lane = lax.broadcasted_iota(jnp.int32, (half, depth), 1)
    for j in range(cands):
        by_real = t_buf[pl.ds(j * width, half), :]
        by_imag = pltpu.roll(t_buf[pl.ds(j * width + half, half), :], cycles, 1)
        pair = by_real + jnp.where(lane < cycles, -by_imag, by_imag)
        turned = pair.T.astype(jnp.bfloat16)
        numer_ref[j, :, :half] = turned[:cycles]
        numer_ref[j, :, half:] = turned[cycles:]


def block_terms(freq_major, noise, chosen):
    half, rows, depth = freq_major.shape
    cands, cycles, width = chosen.shape
    q_real, q_imag = chosen[:, :, :half], chosen[:, :, half:]
    q_both = jnp.stack(
        [
            jnp.concatenate([q_real, q_imag], axis=1),
            jnp.concatenate([-q_imag, q_real], axis=1),
        ],
        axis=1,
    )
    q_major = q_both.transpose(3, 0, 1, 2).reshape(half, 2 * cands, depth)
    cosine, sine = angle_tables(half, width)
    from_freqs = np.concatenate([cosine.T, -sine.T], axis=1)
    to_freqs = np.concatenate([cosine, sine], axis=0)
    wide = chosen.astype(jnp.float32)
    half_norm = 0.5 * jnp.sum(wide * wide, axis=(1, 2))
    half_norm = jnp.broadcast_to(half_norm[:, None], (cands, rows))
    vmem = pl.BlockSpec(memory_space=pltpu.VMEM)
    numerator, weight = pl.pallas_call(
        terms_kernel,
        out_shape=(
            jax.ShapeDtypeStruct((cands, cycles, width), jnp.bfloat16),
            jax.ShapeDtypeStruct((cands, 128), jnp.float32),
        ),
        in_specs=[pl.BlockSpec(memory_space=pltpu.HBM)] + [vmem] * 5,
        out_specs=(vmem, vmem),
        scratch_shapes=[
            pltpu.VMEM(freq_major.shape, freq_major.dtype),
            pltpu.VMEM((rows // 128, cands * width, 128), jnp.float32),
            pltpu.VMEM((cands * width, depth), jnp.float32),
            pltpu.SemaphoreType.DMA((8,)),
        ],
        compiler_params=pltpu.CompilerParams(vmem_limit_bytes=52 * 2**20),
        name="terms",
    )(freq_major, q_major, from_freqs, to_freqs, noise.reshape(1, rows), half_norm)
    return numerator, weight[:, 0]


def local(n_grp, n_rep, particles, noise_var, references, class_order, candidates):
    total = n_grp * n_rep
    cands = candidates.shape[1]
    owned, share, width = references.shape
    cycles = particles.shape[1]
    order = class_order.reshape(1, n_grp * owned)
    got, slots, freq_major = fetch(candidates, order, references, particles, n_rep, total)
    chosen = got.reshape(n_grp, n_rep, OWN, share, width).transpose(0, 2, 1, 3, 4)
    chosen = chosen.reshape(n_grp * OWN, cycles, width)
    spread = None
    if n_grp * OWN != cands:
        held = (class_order[:, None] == candidates.reshape(-1)[None, :]).any(axis=1)
        live = jnp.repeat(held.reshape(n_grp, owned).any(axis=1), OWN)
        place = jnp.cumsum(live.astype(jnp.int32)) - 1
        spread = (
            (place[None, :] == jnp.arange(cands)[:, None]) & live[None, :]
        ).astype(jnp.bfloat16)
        chosen = jnp.einsum(
            "js,srk->jrk", spread, chosen, preferred_element_type=jnp.float32
        ).astype(jnp.bfloat16)
    numerator, weight = block_terms(freq_major, noise_var, chosen)
    if spread is not None:
        numerator = jnp.einsum(
            "js,jrk->srk", spread, numerator, preferred_element_type=jnp.float32
        ).astype(jnp.bfloat16)
        weight = jnp.sum(spread.astype(jnp.float32) * weight[:, None], axis=0)
    parts = numerator.reshape(n_grp, OWN, n_rep, share, width).transpose(0, 2, 1, 3, 4)
    wide_weight = jnp.pad(weight.reshape(n_grp, 1, OWN), ((0, 0), (0, 0), (0, 128 - OWN)))
    back, back_weight = give_back(parts, wide_weight, n_rep, total)
    slot_of = slots[:, :OWN].reshape(-1)
    pick = jnp.arange(owned, dtype=jnp.int32)[:, None] == slot_of[None, :]
    class_sums = jnp.einsum(
        "sb,brk->srk",
        pick.astype(jnp.bfloat16),
        back.reshape(total * OWN, share, width),
        preferred_element_type=jnp.float32,
    )
    own_slot = jnp.arange(owned, dtype=jnp.int32)[:, None]
    class_weights = sum(
        jnp.sum(
            jnp.where(own_slot == slots[None, :, i], back_weight[None, :, 0, i], 0.0), axis=1
        )
        for i in range(OWN)
    )
    return class_sums, class_weights


def solution(mesh):
    placed = (
        P(("grp", "rep"), None, None),
        P(("grp", "rep")),
        P("grp", "rep", None),
        P(),
        P(("grp", "rep"), None),
    )
    return jax.shard_map(
        functools.partial(local, mesh.shape["grp"], mesh.shape["rep"]),
        mesh=mesh,
        in_specs=placed,
        out_specs=(P("grp", "rep", None), P("grp")),
        check_vma=False,
    )
```

profile of v0, /device:TPU:0, one launch (start us, length us, event | category | flops | bytes accessed | tf_op | source)
XLA Modules:
  0.0 65.3 jit_solution(10395842469731271135)
XLA Ops:
  0.6 0.0 copy-start
  0.6 0.0 copy-start.1
  0.7 0.0 copy-start.2
  0.7 26.9 %fetch.1 = (bf16[32,2,8,256]{3,2,1,0:T(8,128)(2,1)}, s32[32,128]{1,0:T(8,128)}, bf16[128,256,128]{2,1,0:T(8,128)(2,1)}) custom-call(s32[1,8]{1,0:T(1,128)} %cand_ref.1, s32[1,200]{1,0:T(1,128)} %bitcast.34, bf16[50,8,256]{2,1,0:T(8,128)(2,1)} %refs_ref.1, bf16[256,64,256]{2,1,0:T(8,128)(2,1)} %rows_ref.1), custom_call_target="tpu_custom_call" | custom-call | tf_op jit(solution)/shard_map/fetch/pallas_call | solution.py:205
  27.6 0.8 %eq.46 = s32[64]{0:T(128)S(1)} reshape(s32[32,2]{1,0:T(8,128)} %bitcast.32) | data formatting | bytes 512 | tf_op jit(solution)/shard_map/eq | solution.py:472
  28.4 1.0 %slice_reduce_fusion.1 = (s32[32]{0:T(128)S(1)}, s32[32]{0:T(128)S(1)}) fusion(s32[32,128]{1,0:T(8,128)} %get-tuple-element.9), kind=kLoop, calls=%fused_computation.11 | loop fusion | bytes 512 | tf_op jit(solution)/shard_map/slice | solution.py:482
  29.4 1.1 %multiply_reduce_fusion = f32[4,2]{1,0:T(4,128)S(1)} fusion(bf16[4,8,2,8,256]{4,3,2,1,0:T(8,128)(2,1)} %bitcast.29), kind=kLoop, calls=%fused_computation.1 | loop fusion | flops 393208 | bytes 262176 | tf_op jit(solution)/shard_map/reduce_sum | solution.py:419
  30.5 1.0 %copy.20 = bf16[4,8,2,8,256]{4,3,1,2,0:T(8,128)(2,1)S(1)} copy(bf16[4,8,2,8,256]{4,3,2,1,0:T(8,128)(2,1)} %bitcast.30) | data formatting | bytes 524288 | tf_op jit(solution)/shard_map/reshape | solution.py:449
  31.5 0.1 mul.16
  31.6 0.1 broadcast_in_dim.30.norm_ref
  31.7 0.1 maximum_bitcast_fusion.1
  31.8 0.1 maximum_bitcast_fusion
  31.9 0.5 copy.21
  32.4 13.0 %terms.1 = (bf16[8,64,256]{2,1,0:T(8,128)(2,1)S(1)}, f32[8,128]{1,0:T(8,128)S(1)}) custom-call(bf16[128,256,128]{2,1,0:T(8,128)(2,1)} %get-tuple-element.10.major_ref, bf16[128,16,128]{2,1,0:T(8,128)(2,1)S(1)} %bitcast.24, f32[256,256]{1,0:T(8,128)S(1)} %copy-done.1, f32[256,256]{1,0:T(8,128)S(1)} %copy-done, f32[1,256]{1,0:T(1,128)S(1)} %bitcast.26, ...), custom_call_target="tpu_custom_call" | custom-call | tf_op jit(solution)/shard_map/terms/pallas_call | solution.py:422
  45.5 0.7 %copy.30 = bf16[4,2,8,8,256]{4,3,1,2,0:T(8,128)(2,1)} copy(bf16[4,2,8,8,256]{4,3,2,1,0:T(8,128)(2,1)S(1)} %bitcast.25) | data formatting | bytes 524288 | tf_op jit(solution)/shard_map/reshape | solution.py:468
  46.2 0.1 slice_reduce_fusion.4
  46.3 0.1 reshape_squeeze.3
  46.4 0.6 pad.4.weight_ref
  47.0 14.3 %give_back.1 = (bf16[32,2,8,256]{3,2,1,0:T(8,128)(2,1)}, f32[32,1,128]{2,1,0:T(1,128)}) custom-call(bf16[4,8,2,8,256]{4,3,2,1,0:T(8,128)(2,1)} %bitcast.28, f32[4,1,128]{2,1,0:T(1,128)} %pad.4.weight_ref), custom_call_target="tpu_custom_call" | custom-call | tf_op jit(solution)/shard_map/give_back/pallas_call | solution.py:280
  61.2 1.4 %slice_reduce_fusion = (f32[32]{0:T(128)S(1)}, f32[32]{0:T(128)S(1)}) fusion(f32[32,1,128]{2,1,0:T(1,128)} %get-tuple-element.15), kind=kLoop, calls=%fused_computation.10 | loop fusion | bytes 512 | tf_op jit(solution)/shard_map/slice | solution.py:482
  62.6 0.1 select_reduce_fusion
  62.7 0.5 add.5
  63.2 1.1 %fusion = f32[50,8,256]{2,0,1:T(8,128)S(1)} fusion(bf16[64,8,256]{2,1,0:T(8,128)(2,1)} %bitcast.31, s32[64]{0:T(128)S(1)} %eq.46), kind=kOutput, calls=%fused_computation.4 | convolution fusion | flops 13110400 | bytes 672000 | tf_op jit(solution)/shard_map/sb,brk->srk/dot_general | solution.py:473
  64.4 0.9 %copy.25 = f32[50,8,256]{2,1,0:T(8,128)} copy(f32[50,8,256]{2,0,1:T(8,128)S(1)} %fusion) | data formatting | bytes 819200
  (5 shorter events, 0.0 us)
Async XLA Ops:
  0.6 31.7 %copy-start = (f32[256,256]{1,0:T(8,128)S(1)}, f32[256,256]{1,0:T(8,128)}, u32[]{:S(2)}) copy-start(f32[256,256]{1,0:T(8,128)} %constant.11.clone.freqs_ref) | copy-start | bytes 786436
  0.6 31.7 %copy-start.1 = (f32[256,256]{1,0:T(8,128)S(1)}, f32[256,256]{1,0:T(8,128)}, u32[]{:S(2)}) copy-start(f32[256,256]{1,0:T(8,128)} %constant.10.clone.angles_ref) | copy-start | bytes 786436
  0.7 31.7 %copy-start.2 = (f32[256]{0:T(256)S(1)}, f32[256]{0:T(256)}, u32[]{:S(2)}) copy-start(f32[256]{0:T(256)} %param.8) | copy-start | bytes 3076
where the time goes:
time: 66 us; the launch traced here: 65.3 us
  Pallas kernels  54.3 us (82%)
  local copies, waits for them, and re-layouts  7.2 us (11%)
  other arithmetic  1.91 us (3%)
  matrix products  1.15 us (2%)
  between operations  0.76 us (1%)
    pallas_call x1, Pallas kernels, fetch(): pl.pallas_call(functools.partial(fetch_kernel, n_rep, total), out_shape=(...  26.9 us
    pallas_call x1, Pallas kernels, give_back(): pl.pallas_call(functools.partial(return_kernel, n_rep, total), out_shape=...  14.3 us
    pallas_call x1, Pallas kernels, block_terms(): pl.pallas_call(terms_kernel, out_shape=(jax.ShapeDtypeStruct((cands, cycl...  13 us
    slice x1, local copies, waits for them, and re-layouts, local(): back_weight[None, :, 0, i]  1.36 us

commit v1 on v0

--- a/solution.py
+++ b/solution.py
@@ -11,6 +11,7 @@
 
 precise = lax.Precision.HIGHEST
 GROUP = 16
+PITCH = GROUP + 4
 OWN = 2
 
 
@@ -18,6 +19,11 @@
     product = np.arange(freq_count)[:, None] * np.arange(angle_count)[None, :] % angle_count
     phase_angle = product * (2.0 * math.pi / angle_count)
     return np.cos(phase_angle).astype(np.float32), np.sin(phase_angle).astype(np.float32)
+
+
+def table_parts(table):
+    high = table.astype(jnp.bfloat16)
+    return high, (table - high.astype(np.float32)).astype(jnp.bfloat16)
 
 
 def peer_of(step, n_rep, total):
@@ -91,8 +97,9 @@
             both = jnp.concatenate(
                 [in_buf[slot, p, :, :half], in_buf[slot, p, :, half:]], axis=0
             )
-            mid_buf[pl.ds(p, half, stride=GROUP), :] = both.T.astype(jnp.float32)
-        out_buf[slot] = mid_buf[...].reshape(out_buf.shape[1:]).astype(out_buf.dtype)
+            mid_buf[pl.ds(p, half, stride=PITCH), :] = both.T.astype(jnp.float32)
+        for k in range(half):
+            out_buf[slot, k] = mid_buf[pl.ds(k * PITCH, GROUP), :].astype(out_buf.dtype)
         store(block).start()
 
     store(stop - 2).wait()
@@ -223,7 +230,7 @@
             pltpu.SemaphoreType.DMA((total,)),
             pltpu.SemaphoreType.DMA((1,)),
             pltpu.VMEM((2, GROUP, depth, full), rows.dtype),
-            pltpu.VMEM((half * GROUP, 2 * depth), jnp.float32),
+            pltpu.VMEM((half * PITCH, 2 * depth), jnp.float32),
             pltpu.VMEM((2, half, GROUP, 2 * depth), rows.dtype),
             pltpu.SemaphoreType.DMA((2,)),
             pltpu.SemaphoreType.DMA((2,)),
@@ -309,8 +316,10 @@
 def terms_kernel(
     major_ref,
     q_ref,
-    angles_ref,
-    freqs_ref,
+    angles_high_ref,
+    angles_low_ref,
+    freqs_high_ref,
+    freqs_low_ref,
     noise_ref,
     norm_ref,
     numer_ref,
@@ -323,13 +332,16 @@
     half, rows, depth = major_ref.shape
     both = q_ref.shape[1]
     cands = both // 2
-    width = 2 * half
     cycles = depth // 2
     chunks = x_sem.shape[0]
     span = half // chunks
+    pitch = half + 4
 
     lanes = f_buf.shape[2]
     tiles = range(f_buf.shape[0])
+
+    def spread(k):
+        return pl.ds(k, both, stride=pitch)
 
     def take(part):
         return jnp.concatenate([f_buf[t, part, :] for t in tiles], axis=1)
@@ -337,6 +349,15 @@
     def put(part, value):
         for t in tiles:
             f_buf[t, part, :] = value[:, t * lanes : (t + 1) * lanes]
+
+    def take_pair(j):
+        return jnp.concatenate(
+            [take(pl.ds((2 * j + c) * pitch, half)) for c in range(2)], axis=0
+        )
+
+    def put_pair(j, value):
+        for c in range(2):
+            put(pl.ds((2 * j + c) * pitch, half), value[c * half : (c + 1) * half])
 
     def chunk_copy(chunk):
         part = pl.ds(chunk * span, span)
@@ -356,44 +377,47 @@
                 (((1,), (1,)), ((), ())),
                 preferred_element_type=jnp.float32,
             )
-            put(pl.ds(k, both, stride=half), found)
+            put(spread(k), found)
 
     inv_noise = 1.0 / noise_ref[...]
     top = jnp.full((1, rows), -jnp.inf, jnp.float32)
     for j in range(cands):
-        part = pl.ds(j * width, width)
-        correlation = dot_wide(angles_ref[...], take(part), precise)
+        high, low = split_wide(take_pair(j))
+        correlation = (
+            dot_wide(angles_high_ref[...], high)
+            + dot_wide(angles_low_ref[...], high)
+            + dot_wide(angles_high_ref[...], low)
+        )
         logits = (correlation - norm_ref[j : j + 1, :]) * inv_noise
-        put(part, logits)
+        put_pair(j, logits)
         top = jnp.maximum(top, jnp.max(logits, axis=0, keepdims=True))
 
     sums = []
     for j in range(cands):
-        part = pl.ds(j * width, width)
-        exponent = jnp.exp(take(part) - top)
-        put(part, exponent)
+        exponent = jnp.exp(take_pair(j) - top)
+        put_pair(j, exponent)
         sums.append(jnp.sum(exponent, axis=0, keepdims=True))
     inv_sum = 1.0 / sum(sums)
-    freqs_high, freqs_low = split_wide(freqs_ref[...])
     for j in range(cands):
-        part = pl.ds(j * width, width)
         weight = jnp.sum(sums[j] * inv_sum, axis=1, keepdims=True)
         weight_ref[j : j + 1, :] = jnp.broadcast_to(weight, (1, weight_ref.shape[1]))
-        high, low = split_wide(take(part) * inv_sum)
-        put(
-            part,
-            dot_wide(freqs_high, high) + dot_wide(freqs_low, high) + dot_wide(freqs_high, low),
+        high, low = split_wide(take_pair(j) * inv_sum)
+        put_pair(
+            j,
+            dot_wide(freqs_high_ref[...], high)
+            + dot_wide(freqs_low_ref[...], high)
+            + dot_wide(freqs_high_ref[...], low),
         )
 
     @pl.loop(0, half, unroll=8)
     def _(k):
-        spectra = take(pl.ds(k, both, stride=half)).astype(jnp.bfloat16)
-        t_buf[pl.ds(k, both, stride=half), :] = dot_wide(spectra, x_buf[k])
+        spectra = take(spread(k)).astype(jnp.bfloat16)
+        t_buf[spread(k), :] = dot_wide(spectra, x_buf[k])
 
     lane = lax.broadcasted_iota(jnp.int32, (half, depth), 1)
     for j in range(cands):
-        by_real = t_buf[pl.ds(j * width, half), :]
-        by_imag = pltpu.roll(t_buf[pl.ds(j * width + half, half), :], cycles, 1)
+        by_real = t_buf[pl.ds(2 * j * pitch, half), :]
+        by_imag = pltpu.roll(t_buf[pl.ds((2 * j + 1) * pitch, half), :], cycles, 1)
         pair = by_real + jnp.where(lane < cycles, -by_imag, by_imag)
         turned = pair.T.astype(jnp.bfloat16)
         numer_ref[j, :, :half] = turned[:cycles]
@@ -425,17 +449,24 @@
             jax.ShapeDtypeStruct((cands, cycles, width), jnp.bfloat16),
             jax.ShapeDtypeStruct((cands, 128), jnp.float32),
         ),
-        in_specs=[pl.BlockSpec(memory_space=pltpu.HBM)] + [vmem] * 5,
+        in_specs=[pl.BlockSpec(memory_space=pltpu.HBM)] + [vmem] * 7,
         out_specs=(vmem, vmem),
         scratch_shapes=[
             pltpu.VMEM(freq_major.shape, freq_major.dtype),
-            pltpu.VMEM((rows // 128, cands * width, 128), jnp.float32),
-            pltpu.VMEM((cands * width, depth), jnp.float32),
+            pltpu.VMEM((rows // 128, 2 * cands * (half + 4), 128), jnp.float32),
+            pltpu.VMEM((2 * cands * (half + 4), depth), jnp.float32),
             pltpu.SemaphoreType.DMA((8,)),
         ],
         compiler_params=pltpu.CompilerParams(vmem_limit_bytes=52 * 2**20),
         name="terms",
-    )(freq_major, q_major, from_freqs, to_freqs, noise.reshape(1, rows), half_norm)
+    )(
+        freq_major,
+        q_major,
+        *table_parts(from_freqs),
+        *table_parts(to_freqs),
+        noise.reshape(1, rows),
+        half_norm,
+    )
     return numerator, weight[:, 0]
 
 

time: 66 us -> 62.8 us (0.952)
  Pallas kernels: 54.3 us -> 51.1 us
    pallas_call x1, Pallas kernels: 13 us -> 11.2 us  [block_terms(): pl.pallas_call(terms_kernel, out_shape=(jax.ShapeDtypeStruct((cands, cycl...]
    pallas_call x1, Pallas kernels: 26.9 us -> 25.6 us  [fetch(): pl.pallas_call(functools.partial(fetch_kernel, n_rep, total), out_shape=(...]
where the time goes in v1:
time: 62.8 us; the launch traced here: 62.1 us
  Pallas kernels  51.1 us (81%)
  local copies, waits for them, and re-layouts  7.21 us (11%)
  other arithmetic  1.91 us (3%)
  matrix products  1.15 us (2%)
  between operations  0.79 us (1%)
    pallas_call x1, Pallas kernels, fetch(): pl.pallas_call(functools.partial(fetch_kernel, n_rep, total), out_shape=(...  25.6 us
    pallas_call x1, Pallas kernels, give_back(): pl.pallas_call(functools.partial(return_kernel, n_rep, total), out_shape=...  14.3 us
    pallas_call x1, Pallas kernels, block_terms(): pl.pallas_call(terms_kernel, out_shape=(jax.ShapeDtypeStruct((cands, cycl...  11.2 us
    slice x1, local copies, waits for them, and re-layouts, local(): back_weight[None, :, 0, i]  1.36 us

profile of v1, /device:TPU:0, one launch (start us, length us, event | category | flops | bytes accessed | tf_op | source)
XLA Modules:
  0.0 62.1 jit_solution(14094054237824854092)
XLA Ops:
  0.6 0.0 copy-start
  0.6 0.0 copy-start.1
  0.7 0.0 copy-start.2
  0.7 25.6 %fetch.1 = (bf16[32,2,8,256]{3,2,1,0:T(8,128)(2,1)}, s32[32,128]{1,0:T(8,128)}, bf16[128,256,128]{2,1,0:T(8,128)(2,1)}) custom-call(s32[1,8]{1,0:T(1,128)} %cand_ref.1, s32[1,200]{1,0:T(1,128)} %bitcast.34, bf16[50,8,256]{2,1,0:T(8,128)(2,1)} %refs_ref.1, bf16[256,64,256]{2,1,0:T(8,128)(2,1)} %rows_ref.1), custom_call_target="tpu_custom_call" | custom-call | tf_op jit(solution)/shard_map/fetch/pallas_call | solution.py:212
  26.3 0.8 %eq.46 = s32[64]{0:T(128)S(1)} reshape(s32[32,2]{1,0:T(8,128)} %bitcast.32) | data formatting | bytes 512 | tf_op jit(solution)/shard_map/eq | solution.py:503
  27.1 1.0 %slice_reduce_fusion.1 = (s32[32]{0:T(128)S(1)}, s32[32]{0:T(128)S(1)}) fusion(s32[32,128]{1,0:T(8,128)} %get-tuple-element.9), kind=kLoop, calls=%fused_computation.11 | loop fusion | bytes 512 | tf_op jit(solution)/shard_map/slice | solution.py:513
  28.1 1.1 %multiply_reduce_fusion = f32[4,2]{1,0:T(4,128)S(1)} fusion(bf16[4,8,2,8,256]{4,3,2,1,0:T(8,128)(2,1)} %bitcast.29), kind=kLoop, calls=%fused_computation.1 | loop fusion | flops 393208 | bytes 262176 | tf_op jit(solution)/shard_map/reduce_sum | solution.py:443
  29.2 1.0 %copy.22 = bf16[4,8,2,8,256]{4,3,1,2,0:T(8,128)(2,1)S(1)} copy(bf16[4,8,2,8,256]{4,3,2,1,0:T(8,128)(2,1)} %bitcast.30) | data formatting | bytes 524288 | tf_op jit(solution)/shard_map/reshape | solution.py:480
  30.2 0.1 mul.16
  30.3 0.1 broadcast_in_dim.30.norm_ref
  30.4 0.1 maximum_bitcast_fusion.1
  30.5 0.1 maximum_bitcast_fusion
  30.5 0.5 copy.23
  31.1 11.2 %terms.1 = (bf16[8,64,256]{2,1,0:T(8,128)(2,1)S(1)}, f32[8,128]{1,0:T(8,128)S(1)}) custom-call(bf16[128,256,128]{2,1,0:T(8,128)(2,1)} %get-tuple-element.10.major_ref, bf16[128,16,128]{2,1,0:T(8,128)(2,1)S(1)} %bitcast.24, bf16[256,256]{1,0:T(8,128)(2,1)S(1)} %copy-done.3, bf16[256,256]{1,0:T(8,128)(2,1)S(1)} %copy-done.2, bf16[256,256]{1,0:T(8,128)(2,1)S(1)} %copy-done.1, ...), custom_call_target="tpu_custom_call" | custom-call | tf_op jit(solution)/shard_map/terms/pallas_call | solution.py:446
  42.3 0.7 %copy.32 = bf16[4,2,8,8,256]{4,3,1,2,0:T(8,128)(2,1)} copy(bf16[4,2,8,8,256]{4,3,2,1,0:T(8,128)(2,1)S(1)} %bitcast.25) | data formatting | bytes 524288 | tf_op jit(solution)/shard_map/reshape | solution.py:499
  43.1 0.1 slice_reduce_fusion.4
  43.2 0.1 reshape_squeeze.3
  43.3 0.6 pad.4.weight_ref
  43.8 14.3 %give_back.1 = (bf16[32,2,8,256]{3,2,1,0:T(8,128)(2,1)}, f32[32,1,128]{2,1,0:T(1,128)}) custom-call(bf16[4,8,2,8,256]{4,3,2,1,0:T(8,128)(2,1)} %bitcast.28, f32[4,1,128]{2,1,0:T(1,128)} %pad.4.weight_ref), custom_call_target="tpu_custom_call" | custom-call | tf_op jit(solution)/shard_map/give_back/pallas_call | solution.py:287
  58.1 1.4 %slice_reduce_fusion = (f32[32]{0:T(128)S(1)}, f32[32]{0:T(128)S(1)}) fusion(f32[32,1,128]{2,1,0:T(1,128)} %get-tuple-element.15), kind=kLoop, calls=%fused_computation.10 | loop fusion | bytes 512 | tf_op jit(solution)/shard_map/slice | solution.py:513
  59.5 0.1 select_reduce_fusion
  59.6 0.5 add.5
  60.1 1.1 %fusion = f32[50,8,256]{2,0,1:T(8,128)S(1)} fusion(bf16[64,8,256]{2,1,0:T(8,128)(2,1)} %bitcast.31, s32[64]{0:T(128)S(1)} %eq.46), kind=kOutput, calls=%fused_computation.4 | convolution fusion | flops 13110400 | bytes 672000 | tf_op jit(solution)/shard_map/sb,brk->srk/dot_general | solution.py:504
  61.3 0.9 %copy.27 = f32[50,8,256]{2,1,0:T(8,128)} copy(f32[50,8,256]{2,0,1:T(8,128)S(1)} %fusion) | data formatting | bytes 819200
  (9 shorter events, 0.1 us)
Async XLA Ops:
  0.6 30.4 %copy-start = (bf16[256,256]{1,0:T(8,128)(2,1)S(1)}, bf16[256,256]{1,0:T(8,128)(2,1)}, u32[]{:S(2)}) copy-start(bf16[256,256]{1,0:T(8,128)(2,1)} %constant.17.clone.freqs_low_ref) | copy-start | bytes 393220
  0.6 30.4 %copy-start.1 = (bf16[256,256]{1,0:T(8,128)(2,1)S(1)}, bf16[256,256]{1,0:T(8,128)(2,1)}, u32[]{:S(2)}) copy-start(bf16[256,256]{1,0:T(8,128)(2,1)} %constant.16.clone.freqs_high_ref) | copy-start | bytes 393220
  0.7 30.4 %copy-start.2 = (bf16[256,256]{1,0:T(8,128)(2,1)S(1)}, bf16[256,256]{1,0:T(8,128)(2,1)}, u32[]{:S(2)}) copy-start(bf16[256,256]{1,0:T(8,128)(2,1)} %constant.15.clone.angles_low_ref) | copy-start | bytes 393220
  0.7 30.4 %copy-start.3 = (bf16[256,256]{1,0:T(8,128)(2,1)S(1)}, bf16[256,256]{1,0:T(8,128)(2,1)}, u32[]{:S(2)}) copy-start(bf16[256,256]{1,0:T(8,128)(2,1)} %constant.14.clone.angles_high_ref) | copy-start | bytes 393220
  0.7 30.4 %copy-start.4 = (f32[256]{0:T(256)S(1)}, f32[256]{0:T(256)}, u32[]{:S(2)}) copy-start(f32[256]{0:T(256)} %param.10) | copy-start | bytes 3076

commit v2 on v1

v2 whole, which is shorter than its diff:
```python
import functools
import math

import jax
import jax.numpy as jnp
import numpy as np
from jax import lax
from jax.experimental import pallas as pl
from jax.experimental.pallas import tpu as pltpu
from jax.sharding import PartitionSpec as P

GROUP = 16
PITCH = GROUP + 4
OWN = 2


def angle_tables(freq_count, angle_count):
    product = np.arange(freq_count)[:, None] * np.arange(angle_count)[None, :] % angle_count
    phase_angle = product * (2.0 * math.pi / angle_count)
    return np.cos(phase_angle).astype(np.float32), np.sin(phase_angle).astype(np.float32)


def table_parts(table):
    high = table.astype(jnp.bfloat16)
    return high, (table - high.astype(np.float32)).astype(jnp.bfloat16)


def peer_of(step, n_rep, total):
    me = lax.axis_index("grp") * n_rep + lax.axis_index("rep")
    peer = lax.rem(me + step, total)
    return peer, {"grp": peer // n_rep, "rep": lax.rem(peer, n_rep)}


def greet_all(n_rep, total):
    barrier = pltpu.get_barrier_semaphore()

    @pl.loop(1, total)
    def _(step):
        _, where = peer_of(step, n_rep, total)
        pl.semaphore_signal(
            barrier, inc=1, device_id=where, device_id_type=pl.DeviceIdType.MESH
        )


def await_all(total):
    pl.semaphore_wait(pltpu.get_barrier_semaphore(), total - 1)


def remote(src, dst, send_sem, recv_sem, where):
    return pltpu.make_async_remote_copy(
        src_ref=src,
        dst_ref=dst,
        send_sem=send_sem,
        recv_sem=recv_sem,
        device_id=where,
        device_id_type=pl.DeviceIdType.MESH,
    )


def split_wide(value):
    high = value.astype(jnp.bfloat16)
    return high, (value - high.astype(jnp.float32)).astype(jnp.bfloat16)


def dot_wide(left, right):
    return jnp.dot(left, right, preferred_element_type=jnp.float32)


def dot_parts(table_high, table_low, value):
    high, low = split_wide(value)
    return dot_wide(table_high, high) + dot_wide(table_low, high) + dot_wide(table_high, low)


def pass_kernel(
    n_rep,
    total,
    cand_ref,
    order_ref,
    noise_ref,
    angles_high_ref,
    angles_low_ref,
    freqs_high_ref,
    freqs_low_ref,
    refs_ref,
    rows_ref,
    sums_ref,
    class_weight_ref,
    cand_pad,
    cand_all,
    slot_vec,
    slot_smem,
    send_buf,
    got_buf,
    in_buf,
    mid_buf,
    x_buf,
    chosen_buf,
    q_buf,
    f_buf,
    t_buf,
    norm_buf,
    turned_buf,
    back_send,
    back_got,
    weight_send,
    weight_got,
    c_send,
    c_recv,
    d_send,
    d_recv,
    s_send,
    s_recv,
    w_send,
    w_recv,
    in_sem,
    l_sem,
):
    grp = lax.axis_index("grp")
    rep = lax.axis_index("rep")
    me = grp * n_rep + rep
    n_grp = total // n_rep
    owned, share, width = refs_ref.shape
    rows, cycles, _ = rows_ref.shape
    half = width // 2
    depth = 2 * cycles
    blocks = rows // GROUP
    cands = n_grp * OWN
    both = 2 * cands
    pitch = half + 4
    q_pitch = both + 4
    message = OWN * share

    def load(block):
        part = pl.ds(block * GROUP, GROUP)
        return pltpu.make_async_copy(rows_ref.at[part], in_buf.at[part], in_sem.at[block])

    @pl.loop(0, blocks)
    def _(block):
        load(block).start()

    cand_pad[...] = jnp.full(cand_pad.shape, -1, jnp.int32)
    cand_pad[:, : cand_ref.shape[1]] = cand_ref[...]
    greet_all(n_rep, total)

    def relayout(start, stop):
        @pl.loop(start, stop)
        def _(block):
            load(block).wait()
            for p in range(GROUP):
                image = in_buf.at[block * GROUP + p]
                turned = jnp.concatenate([image[:, :half], image[:, half:]], axis=0).T
                mid_buf[pl.ds(p, half, stride=PITCH), :] = turned.astype(jnp.float32)
            part = pl.ds(pl.multiple_of(block * GROUP, GROUP), GROUP)
            for k in range(half):
                x_buf[k, part, :] = mid_buf[pl.ds(k * PITCH, GROUP), :].astype(x_buf.dtype)

    cut_one, cut_two = blocks // 4, blocks // 2
    relayout(0, cut_one)
    await_all(total)

    def cand_copy(step, slot):
        _, where = peer_of(step, n_rep, total)
        return remote(cand_pad, cand_all.at[slot], c_send.at[step], c_recv.at[slot], where)

    @pl.loop(1, total)
    def _(step):
        cand_copy(step, me).start()

    cand_all[me] = cand_pad[...]
    relayout(cut_one, cut_two)

    @pl.loop(1, total)
    def _(step):
        cand_copy(step, peer_of(step, n_rep, total)[0]).wait_recv()

    order = order_ref[...]
    slot_no = lax.broadcasted_iota(jnp.int32, (1, order.shape[1]), 1) - grp * owned
    mine = jnp.where((slot_no >= 0) & (slot_no < owned), order, -2)
    wanted = cand_all[...].reshape(total, cand_all.shape[2])
    hit = wanted[:, 0:1] == mine
    for j in range(1, cand_ref.shape[1]):
        hit = jnp.logical_or(hit, wanted[:, j : j + 1] == mine)
    first = jnp.min(jnp.where(hit, slot_no, 2 * owned), axis=1, keepdims=True)
    last = jnp.max(jnp.where(hit, slot_no, -1), axis=1, keepdims=True)
    lane = lax.broadcasted_iota(jnp.int32, slot_vec.shape, 1)
    slot_vec[...] = jnp.where(
        lane == 0, jnp.minimum(first, owned - 1), jnp.maximum(last, 0)
    )
    to_scalar = pltpu.make_async_copy(slot_vec, slot_smem, l_sem.at[0])
    to_scalar.start()
    to_scalar.wait()

    def data_copy(step, block, slot):
        _, where = peer_of(step, n_rep, total)
        return remote(
            send_buf.at[block], got_buf.at[slot], d_send.at[step], d_recv.at[slot], where
        )

    @pl.loop(1, total)
    def _(step):
        peer, _ = peer_of(step, n_rep, total)
        for i in range(OWN):
            send_buf[peer, i] = refs_ref[slot_smem[peer, i]]
        data_copy(step, peer, me).start()

    for i in range(OWN):
        got_buf[me, i] = refs_ref[slot_smem[me, i]]

    relayout(cut_two, blocks)

    live = []
    if cands != cand_ref.shape[1]:
        held = cand_ref[:, 0:1] == order
        for j in range(1, cand_ref.shape[1]):
            held = jnp.logical_or(held, cand_ref[:, j : j + 1] == order)
        slot_all = lax.broadcasted_iota(jnp.int32, order.shape, 1)
        for g in range(n_grp):
            inside = held & (slot_all >= g * owned) & (slot_all < (g + 1) * owned)
            live.append(jnp.max(jnp.where(inside, 1.0, 0.0), axis=1, keepdims=True) > 0.0)

    @pl.loop(1, total)
    def _(step):
        peer, _ = peer_of(step, n_rep, total)
        cand_copy(step, me).wait_send()
        data_copy(step, peer, peer).wait()

    q_lane = lax.broadcasted_iota(jnp.int32, (half, depth), 1)
    for j in range(cands):
        g, i = j // OWN, j % OWN
        for r in range(n_rep):
            chosen_buf[j, pl.ds(r * share, share), :] = got_buf[g * n_rep + r, i].astype(
                jnp.float32
            )
        wide = chosen_buf[j]
        total_square = jnp.sum(jnp.sum(wide * wide, axis=0, keepdims=True), axis=1, keepdims=True)
        norm_buf[j : j + 1, :] = jnp.broadcast_to(0.5 * total_square, (1, rows))
        turned = jnp.concatenate([wide[:, :half], wide[:, half:]], axis=0).T
        q_buf[pl.ds(2 * j, half, stride=q_pitch), :] = turned
        rolled = pltpu.roll(turned, cycles, 1)
        q_buf[pl.ds(2 * j + 1, half, stride=q_pitch), :] = jnp.where(
            q_lane < cycles, -rolled, rolled
        )

    lanes = f_buf.shape[2]
    tiles = range(f_buf.shape[0])

    def spread(k):
        return pl.ds(k, both, stride=pitch)

    def take(part):
        return jnp.concatenate([f_buf[t, part, :] for t in tiles], axis=1)

    def put(part, value):
        for t in tiles:
            f_buf[t, part, :] = value[:, t * lanes : (t + 1) * lanes]

    def take_pair(j):
        return jnp.concatenate(
            [take(pl.ds((2 * j + c) * pitch, half)) for c in range(2)], axis=0
        )

    def put_pair(j, value):
        for c in range(2):
            put(pl.ds((2 * j + c) * pitch, half), value[c * half : (c + 1) * half])

    @pl.loop(0, half, unroll=8)
    def _(k):
        found = lax.dot_general(
            q_buf[pl.ds(k * q_pitch, both), :].astype(jnp.bfloat16),
            x_buf[k],
            (((1,), (1,)), ((), ())),
            preferred_element_type=jnp.float32,
        )
        put(spread(k), found)

    inv_noise = 1.0 / noise_ref[...]
    top = jnp.full((1, rows), -jnp.inf, jnp.float32)
    for j in range(cands):
        correlation = dot_parts(angles_high_ref[...], angles_low_ref[...], take_pair(j))
        logits = (correlation - norm_buf[j : j + 1, :]) * inv_noise
        if live:
            logits = jnp.where(live[j // OWN], logits, -jnp.inf)
        put_pair(j, logits)
        top = jnp.maximum(top, jnp.max(logits, axis=0, keepdims=True))

    sums = []
    for j in range(cands):
        exponent = jnp.exp(take_pair(j) - top)
        put_pair(j, exponent)
        sums.append(jnp.sum(exponent, axis=0, keepdims=True))
    inv_sum = 1.0 / sum(sums)
    w_lane = lax.broadcasted_iota(jnp.int32, (1, weight_send.shape[2]), 1)
    for g in range(n_grp):
        line = jnp.zeros(w_lane.shape, jnp.float32)
        for i in range(OWN):
            weight = jnp.sum(sums[g * OWN + i] * inv_sum, axis=1, keepdims=True)
            line = jnp.where(w_lane == i, weight, line)
        weight_send[g] = line

    def weight_copy(step, slot):
        _, where = peer_of(step, n_rep, total)
        return remote(
            weight_send.at[where["grp"]],
            weight_got.at[slot],
            w_send.at[step],
            w_recv.at[slot],
            where,
        )

    @pl.loop(1, total)
    def _(step):
        weight_copy(step, me).start()

    weight_got[me] = weight_send[grp]

    for j in range(cands):
        put_pair(
            j, dot_parts(freqs_high_ref[...], freqs_low_ref[...], take_pair(j) * inv_sum)
        )

    @pl.loop(0, half, unroll=8)
    def _(k):
        spectra = take(spread(k)).astype(jnp.bfloat16)
        t_buf[spread(k), :] = dot_wide(spectra, x_buf[k])

    def back_copy(g, r, slot):
        where = {"grp": g, "rep": r}
        peer = g * n_rep + r
        return remote(
            back_send.at[peer], back_got.at[slot], s_send.at[peer], s_recv.at[slot], where
        )

    for d in range(n_grp):
        g = lax.rem(grp + d, n_grp)
        for i in range(OWN):
            base = (g * OWN + i) * 2 * pitch
            by_real = t_buf[pl.ds(base, half), :]
            by_imag = pltpu.roll(t_buf[pl.ds(base + pitch, half), :], cycles, 1)
            turned = (by_real + jnp.where(q_lane < cycles, -by_imag, by_imag)).T
            for c in range(2):
                for r in range(n_rep):
                    at = c * cycles + r * share
                    turned_buf[
                        d, pl.ds(r * message + i * share, share), c * half : (c + 1) * half
                    ] = turned[at : at + share]
        for r in range(n_rep):
            back_send[g * n_rep + r] = turned_buf[d, pl.ds(r * message, message), :].astype(
                back_send.dtype
            )

        @pl.loop(0 if d else 1, n_rep)
        def _(step):
            back_copy(g, lax.rem(rep + step, n_rep), me).start()

    back_got[me] = back_send[me]

    shift = share.bit_length() - 1
    pick_row = lax.broadcasted_iota(jnp.int32, (owned * share, total * message), 0)
    pick_lane = lax.broadcasted_iota(jnp.int32, (owned * share, total * message), 1)
    member = lax.broadcasted_iota(jnp.int32, (total, total * message), 1) // share
    block_no = lax.broadcasted_iota(jnp.int32, (total, total * message), 0)
    of_member = jnp.where(member == block_no * OWN, first, 0)
    for i in range(1, OWN):
        of_member = of_member + jnp.where(member == block_no * OWN + i, last, 0)
    of_member = jnp.sum(of_member, axis=0, keepdims=True)
    fits = jnp.logical_and(
        lax.shift_right_logical(pick_row, shift) == of_member,
        ((pick_row ^ pick_lane) & (share - 1)) == 0,
    )
    pick = jnp.where(fits, 1.0, 0.0).astype(jnp.bfloat16)

    @pl.loop(1, total)
    def _(step):
        weight_copy(step, peer_of(step, n_rep, total)[0]).wait()

    got_weight = weight_got[...].reshape(total, weight_got.shape[2])
    w_slot = lax.broadcasted_iota(jnp.int32, got_weight.shape, 1)
    placed = jnp.where(w_slot == first, got_weight[:, 0:1], 0.0)
    placed = placed + jnp.where(w_slot == last, got_weight[:, 1:2], 0.0)
    class_weight_ref[...] = jnp.sum(placed, axis=0, keepdims=True)[:, :owned]

    @pl.loop(1, total)
    def _(step):
        peer, where = peer_of(step, n_rep, total)
        remote(
            back_send.at[peer], back_got.at[peer], s_send.at[peer], s_recv.at[peer], where
        ).wait()

    if message % 16 == 0:
        back = back_got[...].reshape(total * message, width)
    else:
        back = jnp.concatenate(
            [back_got[b].astype(jnp.float32) for b in range(total)], axis=0
        ).astype(jnp.bfloat16)
    sums_ref[...] = dot_wide(pick, back)


def local(n_grp, n_rep, particles, noise_var, references, class_order, candidates):
    total = n_grp * n_rep
    owned, share, width = references.shape
    rows, cycles, _ = particles.shape
    half = width // 2
    depth = 2 * cycles
    cands = n_grp * OWN
    message = OWN * share
    cosine, sine = angle_tables(half, width)
    from_freqs = np.concatenate([cosine.T, -sine.T], axis=1)
    to_freqs = np.concatenate([cosine, sine], axis=0)
    vmem = pl.BlockSpec(memory_space=pltpu.VMEM)
    dma = pltpu.SemaphoreType.DMA
    class_sums, class_weights = pl.pallas_call(
        functools.partial(pass_kernel, n_rep, total),
        out_shape=(
            jax.ShapeDtypeStruct((owned * share, width), jnp.float32),
            jax.ShapeDtypeStruct((1, owned), jnp.float32),
        ),
        in_specs=[vmem] * 8 + [pl.BlockSpec(memory_space=pltpu.HBM)],
        out_specs=(vmem, vmem),
        scratch_shapes=[
            pltpu.VMEM((1, 128), jnp.int32),
            pltpu.VMEM((total, 1, 128), jnp.int32),
            pltpu.VMEM((total, 128), jnp.int32),
            pltpu.SMEM((total, 128), jnp.int32),
            pltpu.VMEM((total, OWN, share, width), references.dtype),
            pltpu.VMEM((total, OWN, share, width), references.dtype),
            pltpu.VMEM(particles.shape, particles.dtype),
            pltpu.VMEM((half * PITCH, depth), jnp.float32),
            pltpu.VMEM((half, rows, depth), particles.dtype),
            pltpu.VMEM((cands, cycles, width), jnp.float32),
            pltpu.VMEM((half * (2 * cands + 4), depth), jnp.float32),
            pltpu.VMEM((rows // 128, 2 * cands * (half + 4), 128), jnp.float32),
            pltpu.VMEM((2 * cands * (half + 4), depth), jnp.float32),
            pltpu.VMEM((cands, rows), jnp.float32),
            pltpu.VMEM((n_grp, n_rep * message, width), jnp.float32),
            pltpu.VMEM((total, message, width), jnp.bfloat16),
            pltpu.VMEM((total, message, width), jnp.bfloat16),
            pltpu.VMEM((n_grp, 1, 128), jnp.float32),
            pltpu.VMEM((total, 1, 128), jnp.float32),
        ]
        + [dma((total,))] * 8
        + [dma((rows // GROUP,)), dma((1,))],
        compiler_params=pltpu.CompilerParams(
            collective_id=0, has_side_effects=True, vmem_limit_bytes=56 * 2**20
        ),
        name="em",
    )(
        candidates,
        class_order.reshape(1, n_grp * owned),
        noise_var.reshape(1, rows),
        *table_parts(from_freqs),
        *table_parts(to_freqs),
        references,
        particles,
    )
    return class_sums.reshape(owned, share, width), class_weights.reshape(owned)


def solution(mesh):
    placed = (
        P(("grp", "rep"), None, None),
        P(("grp", "rep")),
        P("grp", "rep", None),
        P(),
        P(("grp", "rep"), None),
    )
    return jax.shard_map(
        functools.partial(local, mesh.shape["grp"], mesh.shape["rep"]),
        mesh=mesh,
        in_specs=placed,
        out_specs=(P("grp", "rep", None), P("grp")),
        check_vma=False,
    )
```

time: 62.8 us -> 47.4 us (0.75)
  Pallas kernels: 51.1 us -> 43.2 us
  local copies, waits for them, and re-layouts: 7.21 us -> 2.97 us
  other arithmetic: 1.91 us -> 0 us
  matrix products: 1.15 us -> 0 us
    pallas_call x3 -> x1, Pallas kernels: 51.1 us -> 43.2 us  [local(): pl.pallas_call(functools.partial(pass_kernel, n_rep, total), out_shape=(j...]
    slice x3 -> x0, local copies, waits for them, and re-layouts: 2.45 us -> none  [the longest x1 1.36 us: local(): back_weight[None, :, 0, i]]
    unnamed x11 -> x2, local copies, waits for them, and re-layouts: 0.91 us -> 2.97 us
    reshape x2 -> x0, local copies, waits for them, and re-layouts: 1.69 us -> none  [the longest x1 0.97 us: local(): got.reshape(n_grp, n_rep, OWN, share, width).transpose(0, 2, 1, 3, 4)]
    reduce_sum x2 -> x0, other arithmetic: 1.21 us -> none  [the longest x1 1.11 us: block_terms(): half_norm = 0.5 * jnp.sum(wide * wide, axis=(1, 2))]
    dot_general x1 -> x0, matrix products: 1.15 us -> none  [local(): jnp.einsum('sb,brk->srk', pick.astype(jnp.bfloat16), back.reshape(total *...]
    eq x1 -> x0, local copies, waits for them, and re-layouts: 0.82 us -> none  [local(): pick = jnp.arange(owned, dtype=jnp.int32)[:, None] == slot_of[None, :]]
where the time goes in v2:
time: 47.4 us; the launch traced here: 46.8 us
  Pallas kernels  43.2 us (91%)
  local copies, waits for them, and re-layouts  2.97 us (6%)
  between operations  0.64 us (1%)
    pallas_call x1, Pallas kernels, local(): pl.pallas_call(functools.partial(pass_kernel, n_rep, total), out_shape=(j...  43.2 us
    unnamed x2, local copies, waits for them, and re-layouts  2.97 us

profile of v2, /device:TPU:0, one launch (start us, length us, event | category | flops | bytes accessed | tf_op | source)
XLA Modules:
  0.0 46.8 jit_solution(8174775668607741289)
XLA Ops:
  0.6 43.2 %em.1 = (f32[400,256]{1,0:T(8,128)}, f32[1,50]{1,0:T(1,128)}) custom-call(s32[1,8]{1,0:T(1,128)} %cand_ref.1, s32[1,200]{1,0:T(1,128)} %bitcast.5, f32[1,256]{1,0:T(1,128)} %bitcast.6, bf16[256,256]{1,0:T(8,128)(2,1)} %constant.8.clone.angles_high_ref, bf16[256,256]{1,0:T(8,128)(2,1)} %constant.9.clone.angles_low_ref, ...), custom_call_target="tpu_custom_call" | custom-call | tf_op jit(solution)/shard_map/em/pallas_call | solution.py:411
  43.9 1.8 %copy.13 = f32[50,8,256]{2,1,0:T(8,128)} copy(f32[50,8,256]{2,1,0:T(8,128)} %bitcast.4) | data formatting | bytes 819200
  45.6 1.2 %copy.14 = f32[50]{0:T(128)} copy(f32[50]{0:T(128)} %bitcast.7) | data formatting | bytes 400

commit v3 on v2

--- a/solution.py
+++ b/solution.py
@@ -12,6 +12,7 @@
 GROUP = 16
 PITCH = GROUP + 4
 OWN = 2
+LIMIT = 40
 
 
 def angle_tables(freq_count, angle_count):
@@ -25,21 +26,50 @@
     return high, (table - high.astype(np.float32)).astype(jnp.bfloat16)
 
 
+def far_first(rep, n_rep, step):
+    near = jnp.where(2 * rep < n_rep, rep, n_rep - 1 - rep)
+    turn = step - (n_rep - 1 - 2 * near)
+    inner = jnp.where(turn % 2 == 0, turn // 2, 2 * near - turn // 2)
+    target = jnp.where(turn < 0, n_rep - 1 - step, inner)
+    return jnp.where(2 * rep < n_rep, target, n_rep - 1 - target)
+
+
+def each_peer(n_rep, n_grp, action):
+    grp = lax.axis_index("grp")
+    rep = lax.axis_index("rep")
+
+    @pl.loop(0, n_rep)
+    def _(step):
+        to_rep = far_first(rep, n_rep, step)
+        for ahead in range(n_grp - 1, -1, -1):
+            to_grp = lax.rem(grp + ahead, n_grp)
+            if ahead:
+                action(to_grp, to_rep)
+            else:
+
+                @pl.when(to_rep != rep)
+                def _():
+                    action(to_grp, to_rep)
+
+
 def peer_of(step, n_rep, total):
     me = lax.axis_index("grp") * n_rep + lax.axis_index("rep")
     peer = lax.rem(me + step, total)
     return peer, {"grp": peer // n_rep, "rep": lax.rem(peer, n_rep)}
 
 
-def greet_all(n_rep, total):
+def greet_all(n_rep, n_grp):
     barrier = pltpu.get_barrier_semaphore()
 
-    @pl.loop(1, total)
-    def _(step):
-        _, where = peer_of(step, n_rep, total)
+    def greet(to_grp, to_rep):
         pl.semaphore_signal(
-            barrier, inc=1, device_id=where, device_id_type=pl.DeviceIdType.MESH
-        )
+            barrier,
+            inc=1,
+            device_id={"grp": to_grp, "rep": to_rep},
+            device_id_type=pl.DeviceIdType.MESH,
+        )
+
+    each_peer(n_rep, n_grp, greet)
 
 
 def await_all(total):
@@ -74,17 +104,20 @@
 def pass_kernel(
     n_rep,
     total,
+    cand_hbm,
+    order_hbm,
+    noise_hbm,
+    tables_hbm,
+    refs_hbm,
+    rows_ref,
+    back_got,
+    weight_got,
+    slots_ref,
     cand_ref,
     order_ref,
     noise_ref,
-    angles_high_ref,
-    angles_low_ref,
-    freqs_high_ref,
-    freqs_low_ref,
+    tables_ref,
     refs_ref,
-    rows_ref,
-    sums_ref,
-    class_weight_ref,
     cand_pad,
     cand_all,
     slot_vec,
@@ -101,9 +134,7 @@
     norm_buf,
     turned_buf,
     back_send,
-    back_got,
     weight_send,
-    weight_got,
     c_send,
     c_recv,
     d_send,
@@ -134,13 +165,30 @@
         part = pl.ds(block * GROUP, GROUP)
         return pltpu.make_async_copy(rows_ref.at[part], in_buf.at[part], in_sem.at[block])
 
+    pairs = (
+        (cand_hbm, cand_ref),
+        (order_hbm, order_ref),
+        (refs_hbm, refs_ref),
+        (noise_hbm, noise_ref),
+        (tables_hbm, tables_ref),
+    )
+    reads = [
+        pltpu.make_async_copy(src, dst, l_sem.at[n]) for n, (src, dst) in enumerate(pairs)
+    ]
+    reads[0].start()
+    greet_all(n_rep, n_grp)
+    for read in reads[1:3]:
+        read.start()
+
     @pl.loop(0, blocks)
     def _(block):
         load(block).start()
 
+    for read in reads[3:]:
+        read.start()
     cand_pad[...] = jnp.full(cand_pad.shape, -1, jnp.int32)
+    reads[0].wait()
     cand_pad[:, : cand_ref.shape[1]] = cand_ref[...]
-    greet_all(n_rep, total)
 
     def relayout(start, stop):
         @pl.loop(start, stop)
@@ -158,21 +206,23 @@
     relayout(0, cut_one)
     await_all(total)
 
-    def cand_copy(step, slot):
-        _, where = peer_of(step, n_rep, total)
-        return remote(cand_pad, cand_all.at[slot], c_send.at[step], c_recv.at[slot], where)
+    def cand_copy(to_grp, to_rep, slot):
+        where = {"grp": to_grp, "rep": to_rep}
+        peer = to_grp * n_rep + to_rep
+        return remote(cand_pad, cand_all.at[slot], c_send.at[peer], c_recv.at[slot], where)
+
+    each_peer(n_rep, n_grp, lambda g, r: cand_copy(g, r, me).start())
+
+    cand_all[me] = cand_pad[...]
+    relayout(cut_one, cut_two)
 
     @pl.loop(1, total)
     def _(step):
-        cand_copy(step, me).start()
-
-    cand_all[me] = cand_pad[...]
-    relayout(cut_one, cut_two)
-
-    @pl.loop(1, total)
-    def _(step):
-        cand_copy(step, peer_of(step, n_rep, total)[0]).wait_recv()
-
+        peer, where = peer_of(step, n_rep, total)
+        cand_copy(where["grp"], where["rep"], peer).wait_recv()
+
+    reads[1].wait()
+    reads[2].wait()
     order = order_ref[...]
     slot_no = lax.broadcasted_iota(jnp.int32, (1, order.shape[1]), 1) - grp * owned
     mine = jnp.where((slot_no >= 0) & (slot_no < owned), order, -2)
@@ -186,22 +236,25 @@
     slot_vec[...] = jnp.where(
         lane == 0, jnp.minimum(first, owned - 1), jnp.maximum(last, 0)
     )
-    to_scalar = pltpu.make_async_copy(slot_vec, slot_smem, l_sem.at[0])
+    to_scalar = pltpu.make_async_copy(slot_vec, slot_smem, l_sem.at[len(pairs)])
     to_scalar.start()
     to_scalar.wait()
 
-    def data_copy(step, block, slot):
-        _, where = peer_of(step, n_rep, total)
+    def data_copy(to_grp, to_rep, slot):
+        where = {"grp": to_grp, "rep": to_rep}
+        peer = to_grp * n_rep + to_rep
         return remote(
-            send_buf.at[block], got_buf.at[slot], d_send.at[step], d_recv.at[slot], where
-        )
-
-    @pl.loop(1, total)
-    def _(step):
-        peer, _ = peer_of(step, n_rep, total)
+            send_buf.at[peer], got_buf.at[slot], d_send.at[peer], d_recv.at[slot], where
+        )
+
+    def give(to_grp, to_rep):
+        peer = to_grp * n_rep + to_rep
         for i in range(OWN):
             send_buf[peer, i] = refs_ref[slot_smem[peer, i]]
-        data_copy(step, peer, me).start()
+        data_copy(to_grp, to_rep, me).start()
+
+    each_peer(n_rep, n_grp, give)
+    slots_ref[...] = jnp.where(lane == 0, first, last)
 
     for i in range(OWN):
         got_buf[me, i] = refs_ref[slot_smem[me, i]]
@@ -220,9 +273,9 @@
 
     @pl.loop(1, total)
     def _(step):
-        peer, _ = peer_of(step, n_rep, total)
-        cand_copy(step, me).wait_send()
-        data_copy(step, peer, peer).wait()
+        peer, where = peer_of(step, n_rep, total)
+        cand_copy(where["grp"], where["rep"], me).wait_send()
+        data_copy(where["grp"], where["rep"], peer).wait()
 
     q_lane = lax.broadcasted_iota(jnp.int32, (half, depth), 1)
     for j in range(cands):
@@ -273,10 +326,12 @@
         )
         put(spread(k), found)
 
+    reads[3].wait()
+    reads[4].wait()
     inv_noise = 1.0 / noise_ref[...]
     top = jnp.full((1, rows), -jnp.inf, jnp.float32)
     for j in range(cands):
-        correlation = dot_parts(angles_high_ref[...], angles_low_ref[...], take_pair(j))
+        correlation = dot_parts(tables_ref[0], tables_ref[1], take_pair(j))
         logits = (correlation - norm_buf[j : j + 1, :]) * inv_noise
         if live:
             logits = jnp.where(live[j // OWN], logits, -jnp.inf)
@@ -297,26 +352,19 @@
             line = jnp.where(w_lane == i, weight, line)
         weight_send[g] = line
 
-    def weight_copy(step, slot):
-        _, where = peer_of(step, n_rep, total)
+    def weight_copy(to_grp, to_rep, slot):
+        where = {"grp": to_grp, "rep": to_rep}
+        peer = to_grp * n_rep + to_rep
         return remote(
-            weight_send.at[where["grp"]],
-            weight_got.at[slot],
-            w_send.at[step],
-            w_recv.at[slot],
-            where,
-        )
-
-    @pl.loop(1, total)
-    def _(step):
-        weight_copy(step, me).start()
+            weight_send.at[to_grp], weight_got.at[slot], w_send.at[peer], w_recv.at[slot], where
+        )
+
+    each_peer(n_rep, n_grp, lambda g, r: weight_copy(g, r, me).start())
 
     weight_got[me] = weight_send[grp]
 
     for j in range(cands):
-        put_pair(
-            j, dot_parts(freqs_high_ref[...], freqs_low_ref[...], take_pair(j) * inv_sum)
-        )
+        put_pair(j, dot_parts(tables_ref[2], tables_ref[3], take_pair(j) * inv_sum))
 
     @pl.loop(0, half, unroll=8)
     def _(k):
@@ -348,51 +396,65 @@
                 back_send.dtype
             )
 
-        @pl.loop(0 if d else 1, n_rep)
-        def _(step):
-            back_copy(g, lax.rem(rep + step, n_rep), me).start()
-
+    each_peer(n_rep, n_grp, lambda g, r: back_copy(g, r, me).start())
     back_got[me] = back_send[me]
-
-    shift = share.bit_length() - 1
-    pick_row = lax.broadcasted_iota(jnp.int32, (owned * share, total * message), 0)
-    pick_lane = lax.broadcasted_iota(jnp.int32, (owned * share, total * message), 1)
-    member = lax.broadcasted_iota(jnp.int32, (total, total * message), 1) // share
-    block_no = lax.broadcasted_iota(jnp.int32, (total, total * message), 0)
-    of_member = jnp.where(member == block_no * OWN, first, 0)
-    for i in range(1, OWN):
-        of_member = of_member + jnp.where(member == block_no * OWN + i, last, 0)
-    of_member = jnp.sum(of_member, axis=0, keepdims=True)
-    fits = jnp.logical_and(
-        lax.shift_right_logical(pick_row, shift) == of_member,
-        ((pick_row ^ pick_lane) & (share - 1)) == 0,
-    )
-    pick = jnp.where(fits, 1.0, 0.0).astype(jnp.bfloat16)
-
-    @pl.loop(1, total)
-    def _(step):
-        weight_copy(step, peer_of(step, n_rep, total)[0]).wait()
-
-    got_weight = weight_got[...].reshape(total, weight_got.shape[2])
-    w_slot = lax.broadcasted_iota(jnp.int32, got_weight.shape, 1)
-    placed = jnp.where(w_slot == first, got_weight[:, 0:1], 0.0)
-    placed = placed + jnp.where(w_slot == last, got_weight[:, 1:2], 0.0)
-    class_weight_ref[...] = jnp.sum(placed, axis=0, keepdims=True)[:, :owned]
 
     @pl.loop(1, total)
     def _(step):
         peer, where = peer_of(step, n_rep, total)
-        remote(
-            back_send.at[peer], back_got.at[peer], s_send.at[peer], s_recv.at[peer], where
-        ).wait()
-
+        weight_copy(where["grp"], where["rep"], peer).wait()
+        back_copy(where["grp"], where["rep"], peer).wait()
+
+
+def place_kernel(
+    share, back_ref, weight_ref, slots_ref, sums_hbm, class_weight_ref, sums_buf, out_sem
+):
+    total, message, width = back_ref.shape
+    height = sums_buf.shape[0]
+    owned = class_weight_ref.shape[1]
+    chunks = out_sem.shape[0]
+    shift = share.bit_length() - 1
+    slots = slots_ref[...]
+    member = lax.broadcasted_iota(jnp.int32, (total, total * message), 1)
+    member = lax.shift_right_logical(member, shift)
+    block_no = lax.broadcasted_iota(jnp.int32, (total, total * message), 0)
+    of_member = jnp.zeros(member.shape, jnp.int32)
+    for i in range(OWN):
+        of_member = jnp.where(member == block_no * OWN + i, slots[:, i : i + 1], of_member)
+    of_member = jnp.sum(of_member, axis=0, keepdims=True)
     if message % 16 == 0:
-        back = back_got[...].reshape(total * message, width)
+        back = back_ref[...].reshape(total * message, width)
     else:
         back = jnp.concatenate(
-            [back_got[b].astype(jnp.float32) for b in range(total)], axis=0
+            [back_ref[b].astype(jnp.float32) for b in range(total)], axis=0
         ).astype(jnp.bfloat16)
-    sums_ref[...] = dot_wide(pick, back)
+    rows = height // chunks
+    copies = []
+    for chunk in range(chunks):
+        part = pl.ds(chunk * rows, rows)
+        row = lax.broadcasted_iota(jnp.int32, (rows, total * message), 0) + chunk * rows
+        lane = lax.broadcasted_iota(jnp.int32, (rows, total * message), 1)
+        fits = jnp.logical_and(
+            lax.shift_right_logical(row, shift) == of_member,
+            ((row ^ lane) & (share - 1)) == 0,
+        )
+        sums_buf[part, :] = dot_wide(jnp.where(fits, 1.0, 0.0).astype(jnp.bfloat16), back)
+        copy = pltpu.make_async_copy(
+            sums_buf.at[part], sums_hbm.at[part], out_sem.at[chunk]
+        )
+        copy.start()
+        copies.append(copy)
+
+    got_weight = weight_ref[...].reshape(total, weight_ref.shape[2])
+    w_slot = lax.broadcasted_iota(jnp.int32, got_weight.shape, 1)
+    placed = jnp.zeros(got_weight.shape, jnp.float32)
+    for i in range(OWN):
+        placed = placed + jnp.where(
+            w_slot == slots[:, i : i + 1], got_weight[:, i : i + 1], 0.0
+        )
+    class_weight_ref[...] = jnp.sum(placed, axis=0, keepdims=True)[:, :owned]
+    for copy in copies:
+        copy.wait()
 
 
 def local(n_grp, n_rep, particles, noise_var, references, class_order, candidates):
@@ -408,15 +470,23 @@
     to_freqs = np.concatenate([cosine, sine], axis=0)
     vmem = pl.BlockSpec(memory_space=pltpu.VMEM)
     dma = pltpu.SemaphoreType.DMA
-    class_sums, class_weights = pl.pallas_call(
+    hbm = pl.BlockSpec(memory_space=pltpu.HBM)
+    tables = jnp.stack([*table_parts(from_freqs), *table_parts(to_freqs)])
+    back, weights, slots = pl.pallas_call(
         functools.partial(pass_kernel, n_rep, total),
         out_shape=(
-            jax.ShapeDtypeStruct((owned * share, width), jnp.float32),
-            jax.ShapeDtypeStruct((1, owned), jnp.float32),
+            jax.ShapeDtypeStruct((total, message, width), jnp.bfloat16),
+            jax.ShapeDtypeStruct((total, 1, 128), jnp.float32),
+            jax.ShapeDtypeStruct((total, 128), jnp.int32),
         ),
-        in_specs=[vmem] * 8 + [pl.BlockSpec(memory_space=pltpu.HBM)],
-        out_specs=(vmem, vmem),
+        in_specs=[hbm] * 6,
+        out_specs=(vmem, vmem, vmem),
         scratch_shapes=[
+            pltpu.VMEM(candidates.shape, jnp.int32),
+            pltpu.VMEM((1, n_grp * owned), jnp.int32),
+            pltpu.VMEM((1, rows), jnp.float32),
+            pltpu.VMEM((4, width, width), jnp.bfloat16),
+            pltpu.VMEM(references.shape, references.dtype),
             pltpu.VMEM((1, 128), jnp.int32),
             pltpu.VMEM((total, 1, 128), jnp.int32),
             pltpu.VMEM((total, 128), jnp.int32),
@@ -433,25 +503,41 @@
             pltpu.VMEM((cands, rows), jnp.float32),
             pltpu.VMEM((n_grp, n_rep * message, width), jnp.float32),
             pltpu.VMEM((total, message, width), jnp.bfloat16),
-            pltpu.VMEM((total, message, width), jnp.bfloat16),
             pltpu.VMEM((n_grp, 1, 128), jnp.float32),
-            pltpu.VMEM((total, 1, 128), jnp.float32),
         ]
         + [dma((total,))] * 8
-        + [dma((rows // GROUP,)), dma((1,))],
+        + [dma((rows // GROUP,)), dma((6,))],
         compiler_params=pltpu.CompilerParams(
-            collective_id=0, has_side_effects=True, vmem_limit_bytes=56 * 2**20
+            collective_id=0, has_side_effects=True, vmem_limit_bytes=LIMIT * 2**20
         ),
         name="em",
     )(
-        candidates,
-        class_order.reshape(1, n_grp * owned),
-        noise_var.reshape(1, rows),
-        *table_parts(from_freqs),
-        *table_parts(to_freqs),
-        references,
-        particles,
+        *(
+            pltpu.with_memory_space_constraint(array, pltpu.HBM)
+            for array in (
+                candidates,
+                class_order.reshape(1, n_grp * owned),
+                noise_var.reshape(1, rows),
+                tables,
+                references,
+                particles,
+            )
+        )
     )
+    height = owned * share
+    chunks = 2 if height % 16 == 0 else 1
+    class_sums, class_weights = pl.pallas_call(
+        functools.partial(place_kernel, share),
+        out_shape=(
+            jax.ShapeDtypeStruct((height, width), jnp.float32),
+            jax.ShapeDtypeStruct((1, owned), jnp.float32),
+        ),
+        in_specs=[vmem] * 3,
+        out_specs=(hbm, vmem),
+        scratch_shapes=[pltpu.VMEM((height, width), jnp.float32), dma((chunks,))],
+        compiler_params=pltpu.CompilerParams(vmem_limit_bytes=16 * 2**20),
+        name="place",
+    )(back, weights, slots)
     return class_sums.reshape(owned, share, width), class_weights.reshape(owned)
 
 

time: 47.4 us -> 42.1 us (0.89)
  local copies, waits for them, and re-layouts: 2.97 us -> 0 us
  Pallas kernels: 43.2 us -> 41.2 us
    pallas_call x1, Pallas kernels: 43.2 us -> 39.6 us  [local(): pl.pallas_call(functools.partial(pass_kernel, n_rep, total), out_shape=(j...]
    unnamed x2 -> x0, local copies, waits for them, and re-layouts: 2.97 us -> none
    pallas_call x0 -> x1, Pallas kernels: none -> 1.67 us  [local(): pl.pallas_call(functools.partial(place_kernel, share), out_shape=(jax.Sha...]
where the time goes in v3:
time: 42.1 us; the launch traced here: 41.9 us
  Pallas kernels  41.2 us (98%)
  between operations  0.64 us (2%)
    pallas_call x1, Pallas kernels, local(): pl.pallas_call(functools.partial(pass_kernel, n_rep, total), out_shape=(j...  39.6 us
    pallas_call x1, Pallas kernels, local(): pl.pallas_call(functools.partial(place_kernel, share), out_shape=(jax.Sha...  1.67 us

profile of v3, /device:TPU:0, one launch (start us, length us, event | category | flops | bytes accessed | tf_op | source)
XLA Modules:
  0.0 41.9 jit_solution(14289060747224711257)
XLA Ops:
  0.6 39.6 %em.1 = (bf16[32,16,256]{2,1,0:T(8,128)(2,1)S(1)}, f32[32,1,128]{2,1,0:T(1,128)S(1)}, s32[32,128]{1,0:T(8,128)S(1)}) custom-call(s32[1,8]{1,0:T(1,128)} %cand_hbm.1, s32[1,200]{1,0:T(1,128)} %bitcast.4, f32[1,256]{1,0:T(1,128)} %bitcast.5, bf16[4,256,256]{2,1,0:T(8,128)(2,1)} %constant.18.tables_hbm, bf16[50,8,256]{2,1,0:T(8,128)(2,1)} %refs_hbm.1, ...), custom_call_target="tpu_custom_call" | custom-call | tf_op jit(solution)/shard_map/em/pallas_call | solution.py:475
  40.2 1.7 %place.1 = (f32[400,256]{1,0:T(8,128)}, f32[1,50]{1,0:T(1,128)}) custom-call(bf16[32,16,256]{2,1,0:T(8,128)(2,1)S(1)} %get-tuple-element.7.back_ref, f32[32,1,128]{2,1,0:T(1,128)S(1)} %get-tuple-element.8.weight_ref, s32[32,128]{1,0:T(8,128)S(1)} %get-tuple-element.9.slots_ref), custom_call_target="tpu_custom_call" | custom-call | tf_op jit(solution)/shard_map/place/pallas_call | solution.py:529

commit v4 on v3

--- a/solution.py
+++ b/solution.py
@@ -307,42 +307,57 @@
         for t in tiles:
             f_buf[t, part, :] = value[:, t * lanes : (t + 1) * lanes]
 
-    def take_pair(j):
-        return jnp.concatenate(
-            [take(pl.ds((2 * j + c) * pitch, half)) for c in range(2)], axis=0
-        )
-
-    def put_pair(j, value):
-        for c in range(2):
-            put(pl.ds((2 * j + c) * pitch, half), value[c * half : (c + 1) * half])
-
-    @pl.loop(0, half, unroll=8)
-    def _(k):
-        found = lax.dot_general(
-            q_buf[pl.ds(k * q_pitch, both), :].astype(jnp.bfloat16),
-            x_buf[k],
-            (((1,), (1,)), ((), ())),
-            preferred_element_type=jnp.float32,
-        )
-        put(spread(k), found)
+    quarter = half // 2
+
+    def spread_folded(pair, parity):
+        return pl.ds(parity * quarter + pair, both, stride=pitch)
+
+    def folded(j, parity, c):
+        return pl.ds((2 * j + c) * pitch + parity * quarter, quarter)
+
+    def angle_half(j, upper):
+        return pl.ds((2 * j + upper) * pitch, half)
+
+    @pl.loop(0, quarter, unroll=4)
+    def _(pair):
+        for parity in range(2):
+            k = 2 * pair + parity
+            found = lax.dot_general(
+                q_buf[pl.ds(k * q_pitch, both), :].astype(jnp.bfloat16),
+                x_buf[k],
+                (((1,), (1,)), ((), ())),
+                preferred_element_type=jnp.float32,
+            )
+            put(spread_folded(pair, parity), found)
 
     reads[3].wait()
     reads[4].wait()
     inv_noise = 1.0 / noise_ref[...]
     top = jnp.full((1, rows), -jnp.inf, jnp.float32)
     for j in range(cands):
-        correlation = dot_parts(tables_ref[0], tables_ref[1], take_pair(j))
-        logits = (correlation - norm_buf[j : j + 1, :]) * inv_noise
-        if live:
-            logits = jnp.where(live[j // OWN], logits, -jnp.inf)
-        put_pair(j, logits)
-        top = jnp.maximum(top, jnp.max(logits, axis=0, keepdims=True))
+        even, odd = (
+            dot_parts(
+                tables_ref[2 * parity],
+                tables_ref[2 * parity + 1],
+                jnp.concatenate([take(folded(j, parity, c)) for c in range(2)], axis=0),
+            )
+            for parity in range(2)
+        )
+        for upper, correlation in enumerate((even + odd, even - odd)):
+            logits = (correlation - norm_buf[j : j + 1, :]) * inv_noise
+            if live:
+                logits = jnp.where(live[j // OWN], logits, -jnp.inf)
+            put(angle_half(j, upper), logits)
+            top = jnp.maximum(top, jnp.max(logits, axis=0, keepdims=True))
 
     sums = []
     for j in range(cands):
-        exponent = jnp.exp(take_pair(j) - top)
-        put_pair(j, exponent)
-        sums.append(jnp.sum(exponent, axis=0, keepdims=True))
+        part_sum = 0.0
+        for upper in range(2):
+            exponent = jnp.exp(take(angle_half(j, upper)) - top)
+            put(angle_half(j, upper), exponent)
+            part_sum = part_sum + jnp.sum(exponent, axis=0, keepdims=True)
+        sums.append(part_sum)
     inv_sum = 1.0 / sum(sums)
     w_lane = lax.broadcasted_iota(jnp.int32, (1, weight_send.shape[2]), 1)
     for g in range(n_grp):
@@ -364,12 +379,20 @@
     weight_got[me] = weight_send[grp]
 
     for j in range(cands):
-        put_pair(j, dot_parts(tables_ref[2], tables_ref[3], take_pair(j) * inv_sum))
-
-    @pl.loop(0, half, unroll=8)
-    def _(k):
-        spectra = take(spread(k)).astype(jnp.bfloat16)
-        t_buf[spread(k), :] = dot_wide(spectra, x_buf[k])
+        lower, upper = (take(angle_half(j, h)) * inv_sum for h in range(2))
+        for parity, weights in enumerate((lower + upper, lower - upper)):
+            result = dot_parts(
+                tables_ref[4 + 2 * parity], tables_ref[5 + 2 * parity], weights
+            )
+            for c in range(2):
+                put(folded(j, parity, c), result[c * quarter : (c + 1) * quarter])
+
+    @pl.loop(0, quarter, unroll=4)
+    def _(pair):
+        for parity in range(2):
+            k = 2 * pair + parity
+            spectra = take(spread_folded(pair, parity)).astype(jnp.bfloat16)
+            t_buf[spread(k), :] = dot_wide(spectra, x_buf[k])
 
     def back_copy(g, r, slot):
         where = {"grp": g, "rep": r}
@@ -466,12 +489,14 @@
     cands = n_grp * OWN
     message = OWN * share
     cosine, sine = angle_tables(half, width)
-    from_freqs = np.concatenate([cosine.T, -sine.T], axis=1)
-    to_freqs = np.concatenate([cosine, sine], axis=0)
+    cosine, sine = cosine[:, :half], sine[:, :half]
+    parities = [slice(0, None, 2), slice(1, None, 2)]
+    from_freqs = [np.concatenate([cosine[p].T, -sine[p].T], axis=1) for p in parities]
+    to_freqs = [np.concatenate([cosine[p], sine[p]], axis=0) for p in parities]
     vmem = pl.BlockSpec(memory_space=pltpu.VMEM)
     dma = pltpu.SemaphoreType.DMA
     hbm = pl.BlockSpec(memory_space=pltpu.HBM)
-    tables = jnp.stack([*table_parts(from_freqs), *table_parts(to_freqs)])
+    tables = jnp.stack([part for t in from_freqs + to_freqs for part in table_parts(t)])
     back, weights, slots = pl.pallas_call(
         functools.partial(pass_kernel, n_rep, total),
         out_shape=(
@@ -485,7 +510,7 @@
             pltpu.VMEM(candidates.shape, jnp.int32),
             pltpu.VMEM((1, n_grp * owned), jnp.int32),
             pltpu.VMEM((1, rows), jnp.float32),
-            pltpu.VMEM((4, width, width), jnp.bfloat16),
+            pltpu.VMEM((8, half, half), jnp.bfloat16),
             pltpu.VMEM(references.shape, references.dtype),
             pltpu.VMEM((1, 128), jnp.int32),
             pltpu.VMEM((total, 1, 128), jnp.int32),

time: 42.1 us -> 42.1 us (level)
  no operation moved by 1% of the time
where the time goes in v4:
time: 42.1 us; the launch traced here: 41.9 us
  Pallas kernels  41.2 us (98%)
  between operations  0.64 us (2%)
    pallas_call x1, Pallas kernels, local(): pl.pallas_call(functools.partial(pass_kernel, n_rep, total), out_shape=(j...  39.5 us
    pallas_call x1, Pallas kernels, local(): pl.pallas_call(functools.partial(place_kernel, share), out_shape=(jax.Sha...  1.67 us

profile of v4, /device:TPU:0, one launch (start us, length us, event | category | flops | bytes accessed | tf_op | source)
XLA Modules:
  0.0 41.9 jit_solution(7358657046971431486)
XLA Ops:
  0.6 39.5 %em.1 = (bf16[32,16,256]{2,1,0:T(8,128)(2,1)S(1)}, f32[32,1,128]{2,1,0:T(1,128)S(1)}, s32[32,128]{1,0:T(8,128)S(1)}) custom-call(s32[1,8]{1,0:T(1,128)} %cand_hbm.1, s32[1,200]{1,0:T(1,128)} %bitcast.4, f32[1,256]{1,0:T(1,128)} %bitcast.5, bf16[8,128,128]{2,1,0:T(8,128)(2,1)} %constant.34.tables_hbm, bf16[50,8,256]{2,1,0:T(8,128)(2,1)} %refs_hbm.1, ...), custom_call_target="tpu_custom_call" | custom-call | tf_op jit(solution)/shard_map/em/pallas_call | solution.py:500
  40.2 1.7 %place.1 = (f32[400,256]{1,0:T(8,128)}, f32[1,50]{1,0:T(1,128)}) custom-call(bf16[32,16,256]{2,1,0:T(8,128)(2,1)S(1)} %get-tuple-element.7.back_ref, f32[32,1,128]{2,1,0:T(1,128)S(1)} %get-tuple-element.8.weight_ref, s32[32,128]{1,0:T(8,128)S(1)} %get-tuple-element.9.slots_ref), custom_call_target="tpu_custom_call" | custom-call | tf_op jit(solution)/shard_map/place/pallas_call | solution.py:554

commit v5 on v4

--- a/solution.py
+++ b/solution.py
@@ -275,7 +275,12 @@
     def _(step):
         peer, where = peer_of(step, n_rep, total)
         cand_copy(where["grp"], where["rep"], me).wait_send()
-        data_copy(where["grp"], where["rep"], peer).wait()
+        data_copy(where["grp"], where["rep"], peer).wait_send()
+
+    @pl.loop(1, total)
+    def _(step):
+        peer, where = peer_of(step, n_rep, total)
+        data_copy(where["grp"], where["rep"], peer).wait_recv()
 
     q_lane = lax.broadcasted_iota(jnp.int32, (half, depth), 1)
     for j in range(cands):
@@ -426,7 +431,12 @@
     def _(step):
         peer, where = peer_of(step, n_rep, total)
         weight_copy(where["grp"], where["rep"], peer).wait()
-        back_copy(where["grp"], where["rep"], peer).wait()
+        back_copy(where["grp"], where["rep"], peer).wait_send()
+
+    @pl.loop(1, total)
+    def _(step):
+        peer, where = peer_of(step, n_rep, total)
+        back_copy(where["grp"], where["rep"], peer).wait_recv()
 
 
 def place_kernel(

time: 42.1 us -> 41.5 us (0.986)
    pallas_call x1, Pallas kernels: 39.5 us -> 39.1 us  [local(): pl.pallas_call(functools.partial(pass_kernel, n_rep, total), out_shape=(j...]
where the time goes in v5:
time: 41.5 us; the launch traced here: 41.4 us
  Pallas kernels  40.8 us (98%)
  between operations  0.64 us (2%)
    pallas_call x1, Pallas kernels, local(): pl.pallas_call(functools.partial(pass_kernel, n_rep, total), out_shape=(j...  39.1 us
    pallas_call x1, Pallas kernels, local(): pl.pallas_call(functools.partial(place_kernel, share), out_shape=(jax.Sha...  1.67 us

profile of v5, /device:TPU:0, one launch (start us, length us, event | category | flops | bytes accessed | tf_op | source)
XLA Modules:
  0.0 41.4 jit_solution(16729323666938398188)
XLA Ops:
  0.6 39.1 %em.1 = (bf16[32,16,256]{2,1,0:T(8,128)(2,1)S(1)}, f32[32,1,128]{2,1,0:T(1,128)S(1)}, s32[32,128]{1,0:T(8,128)S(1)}) custom-call(s32[1,8]{1,0:T(1,128)} %cand_hbm.1, s32[1,200]{1,0:T(1,128)} %bitcast.4, f32[1,256]{1,0:T(1,128)} %bitcast.5, bf16[8,128,128]{2,1,0:T(8,128)(2,1)} %constant.34.tables_hbm, bf16[50,8,256]{2,1,0:T(8,128)(2,1)} %refs_hbm.1, ...), custom_call_target="tpu_custom_call" | custom-call | tf_op jit(solution)/shard_map/em/pallas_call | solution.py:510
  39.7 1.7 %place.1 = (f32[400,256]{1,0:T(8,128)}, f32[1,50]{1,0:T(1,128)}) custom-call(bf16[32,16,256]{2,1,0:T(8,128)(2,1)S(1)} %get-tuple-element.7.back_ref, f32[32,1,128]{2,1,0:T(1,128)S(1)} %get-tuple-element.8.weight_ref, s32[32,128]{1,0:T(8,128)S(1)} %get-tuple-element.9.slots_ref), custom_call_target="tpu_custom_call" | custom-call | tf_op jit(solution)/shard_map/place/pallas_call | solution.py:564
